TPU v7x, 32 devices: a whole 2x2x4 slice. The times are simulated.
32 devices in a mesh: groups: 2 (over x), ctx: 16 (over z, y, core).
Axes of the slice: x: 2, y: 2, z: 4, core: 2. Of those that a mesh axis runs over, the one named last changes fastest.
Arguments:
- query_video: bfloat16 [12288, 1536], P(('groups', 'ctx')), parts along dimension 0, may hold values from -10 to 10
- key_video: bfloat16 [12288, 1536], P(('groups', 'ctx')), parts along dimension 0, may hold values from -5 to 5
- value_video: bfloat16 [12288, 1536], P(('groups', 'ctx')), parts along dimension 0, may hold values from -6 to 6
- query_text: bfloat16 [512, 1536], P(('groups', 'ctx')), parts along dimension 0, may hold values from -10 to 10
- key_text: bfloat16 [512, 1536], P(('groups', 'ctx')), parts along dimension 0, may hold values from -5 to 5
- value_text: bfloat16 [512, 1536], P(('groups', 'ctx')), parts along dimension 0, may hold values from -6 to 6
- key_tiles: int32 [32, 3], P(('groups', 'ctx')), parts along dimension 0, may hold values from 0 to 15, as said below
- tile_owner: int32 [32], P('groups'), parts along dimension 0, may hold values from 0 to 15, as said below
- text_count: int32 [2], P('groups'), parts along dimension 0, may hold values from 64 to 256
Outputs:
- video_out: bfloat16 [12288, 1536], P(('groups', 'ctx')), parts along dimension 0
- text_out: bfloat16 [512, 1536], P(('groups', 'ctx')), parts along dimension 0
There are 2 independent parts, one for each index of `groups`. A program takes and returns all parts, laid end to end along the dimension named above; each array names one. Nothing has to cross between parts.
Inputs may be any that keep to these rules, and one draw needn't show every extreme that they name: `key_tiles`: each list names 3 different tiles, the query tile itself among them; every listed tile has a stored position whose device (position) is at most 2 away from the query tile's device, and every list names one exactly 2 away. `tile_owner`: A permutation of the tile numbers.
All inputs are finite; a program needn't handle non-finite values.
Results may differ from a plain program's by a relative error of at most 0.0032.
Values may be sent and summed in bfloat16 or wider, within the bound.
A program may use at most 384 MiB of HBM per device.

v0:
```python
import math
import jax
import jax.numpy as jnp
from jax import lax
from jax.sharding import PartitionSpec as P

TILE = 384
HD = 128
NB = 3
REACH = 2


def shifted(shard, axis, by):
    count = lax.axis_size(axis)
    pairs = [(i, i + by) for i in range(count) if 0 <= i + by < count]
    return lax.ppermute(shard, axis, pairs)


def combined_all(value, axis, join):
    pieces = jax.tree.map(lambda part: lax.all_gather(part, axis), value)
    head = jax.tree.map(lambda part: part[0], pieces)
    tail = jax.tree.map(lambda part: part[1:], pieces)
    total, _ = lax.scan(lambda total, share: (join(total, share), None), head, tail)
    return total


def spread_heads(values):
    return jnp.repeat(values, HD, axis=1)


def combine_parts(earlier_part, later_part):
    max_early, total_early, acc_early = earlier_part
    max_late, total_late, acc_late = later_part
    joint_max = jnp.maximum(max_early, max_late)
    factor_early = jnp.exp(max_early - joint_max)
    factor_late = jnp.exp(max_late - joint_max)
    joint_total = total_early * factor_early + total_late * factor_late
    joint_acc = acc_early * spread_heads(factor_early) + acc_late * spread_heads(factor_late)
    return (joint_max, joint_total, joint_acc)


def on_device(
    query_video,
    key_video,
    value_video,
    query_text,
    key_text,
    value_text,
    key_tiles,
    tile_owner,
    text_count,
):
    ctx_rank = lax.axis_index("ctx")
    row_count, feature_width = query_video.shape
    head_count = feature_width // HD
    tiles_here = row_count // TILE
    text_here = query_text.shape[0]
    inverse_root_dimension = 1.0 / math.sqrt(HD)
    text_query, text_keys, text_values = (
        lax.all_gather(query_text, "ctx", axis=0, tiled=True),
        lax.all_gather(key_text, "ctx", axis=0, tiled=True),
        lax.all_gather(value_text, "ctx", axis=0, tiled=True),
    )
    text_rows = text_keys.shape[0]
    text_limit = text_count[0]
    text_ok = jnp.arange(text_rows) < text_limit
    local_ok = ctx_rank * text_here + jnp.arange(text_here) < text_limit
    own_pair = (key_video, value_video)
    fetched = {}
    for offset in [value for value in range(-REACH, REACH + 1) if value != 0]:
        fetched[offset] = shifted((own_pair[0], own_pair[1]), "ctx", -offset)
    fetched[0] = own_pair
    window_keys = jnp.concatenate(
        [fetched[offset][0] for offset in range(-REACH, REACH + 1)], axis=0
    )
    window_values = jnp.concatenate(
        [fetched[offset][1] for offset in range(-REACH, REACH + 1)], axis=0
    )
    window_tiles = (2 * REACH + 1) * tiles_here
    tile_count = tile_owner.shape[0]
    matches = key_tiles[:, :, None] == jnp.arange(tile_count, dtype=jnp.int32)[None, None, :]
    key_slots = jnp.sum(jnp.where(matches, tile_owner[None, None, :], 0), axis=-1)
    window_index = key_slots - (ctx_rank - REACH) * tiles_here

    def head_step(head_index, carry_state):
        video_buffer, text_max, text_sum, text_acc = carry_state
        column_start = head_index * HD
        query_head = lax.dynamic_slice_in_dim(query_video, column_start, HD, 1).reshape(
            tiles_here, TILE, HD
        )
        key_window = lax.dynamic_slice_in_dim(window_keys, column_start, HD, 1).reshape(
            window_tiles, TILE, HD
        )
        value_window = lax.dynamic_slice_in_dim(window_values, column_start, HD, 1).reshape(
            window_tiles, TILE, HD
        )
        key_near = key_window[window_index].reshape(tiles_here, NB * TILE, HD)
        value_near = value_window[window_index].reshape(tiles_here, NB * TILE, HD)
        key_words = lax.dynamic_slice_in_dim(text_keys, column_start, HD, 1)
        value_words = lax.dynamic_slice_in_dim(text_values, column_start, HD, 1)
        frame_affinity_array = (
            jnp.einsum("tqd,tkd->tqk", query_head, key_near, preferred_element_type=jnp.float32)
            * inverse_root_dimension
        )
        wording_affinity_array = (
            jnp.einsum("tqd,kd->tqk", query_head, key_words, preferred_element_type=jnp.float32)
            * inverse_root_dimension
        )
        wording_affinity_array = jnp.where(text_ok[None, None, :], wording_affinity_array, -jnp.inf)
        row_max = jnp.maximum(
            jnp.max(frame_affinity_array, axis=-1, keepdims=True),
            jnp.max(wording_affinity_array, axis=-1, keepdims=True),
        )
        weight_video = jnp.exp(frame_affinity_array - row_max)
        weight_text = jnp.exp(wording_affinity_array - row_max)
        row_total = jnp.sum(weight_video, axis=-1) + jnp.sum(weight_text, axis=-1)
        mixed_values = jnp.einsum(
            "tqk,tkd->tqd",
            weight_video.astype(jnp.bfloat16),
            value_near,
            preferred_element_type=jnp.float32,
        )
        mixed_values = mixed_values + jnp.einsum(
            "tqk,kd->tqd",
            weight_text.astype(jnp.bfloat16),
            value_words,
            preferred_element_type=jnp.float32,
        )
        head_output = (
            (mixed_values / row_total[:, :, None]).astype(jnp.bfloat16).reshape(row_count, HD)
        )
        video_buffer = lax.dynamic_update_slice_in_dim(video_buffer, head_output, column_start, 1)
        text_head = lax.dynamic_slice_in_dim(text_query, column_start, HD, 1)
        key_local = lax.dynamic_slice_in_dim(key_video, column_start, HD, 1)
        value_local = lax.dynamic_slice_in_dim(value_video, column_start, HD, 1)
        key_own_text = lax.dynamic_slice_in_dim(key_text, column_start, HD, 1)
        value_own_text = lax.dynamic_slice_in_dim(value_text, column_start, HD, 1)
        score_local = (
            jnp.einsum("td,kd->tk", text_head, key_local, preferred_element_type=jnp.float32)
            * inverse_root_dimension
        )
        score_own = (
            jnp.einsum("td,kd->tk", text_head, key_own_text, preferred_element_type=jnp.float32)
            * inverse_root_dimension
        )
        score_own = jnp.where(local_ok[None, :], score_own, -jnp.inf)
        block_max = jnp.maximum(jnp.max(score_local, axis=-1), jnp.max(score_own, axis=-1))
        weight_local = jnp.exp(score_local - block_max[:, None])
        weight_own = jnp.exp(score_own - block_max[:, None])
        block_total = jnp.sum(weight_local, axis=-1) + jnp.sum(weight_own, axis=-1)
        block_acc = jnp.einsum(
            "tk,kd->td",
            weight_local.astype(jnp.bfloat16),
            value_local,
            preferred_element_type=jnp.float32,
        )
        block_acc = block_acc + jnp.einsum(
            "tk,kd->td",
            weight_own.astype(jnp.bfloat16),
            value_own_text,
            preferred_element_type=jnp.float32,
        )
        text_max = lax.dynamic_update_slice(text_max, block_max[:, None], (0, head_index))
        text_sum = lax.dynamic_update_slice(text_sum, block_total[:, None], (0, head_index))
        text_acc = lax.dynamic_update_slice_in_dim(text_acc, block_acc, column_start, 1)
        return (video_buffer, text_max, text_sum, text_acc)

    initial_state = (
        jnp.zeros((row_count, feature_width), jnp.bfloat16),
        jnp.zeros((text_rows, head_count), jnp.float32),
        jnp.zeros((text_rows, head_count), jnp.float32),
        jnp.zeros((text_rows, feature_width), jnp.float32),
    )
    video_out, text_max, text_sum, text_acc = lax.fori_loop(0, head_count, head_step, initial_state)
    joint_max, joint_total, joint_acc = combined_all(
        (text_max, text_sum, text_acc), "ctx", combine_parts
    )
    own_total = lax.dynamic_slice_in_dim(joint_total, ctx_rank * text_here, text_here, 0)
    own_acc = lax.dynamic_slice_in_dim(joint_acc, ctx_rank * text_here, text_here, 0)
    text_out = (own_acc / spread_heads(own_total)).astype(jnp.bfloat16)
    return (video_out, text_out)


def solution(mesh):
    return jax.shard_map(
        on_device,
        mesh=mesh,
        in_specs=(
            P(("groups", "ctx"), None),
            P(("groups", "ctx"), None),
            P(("groups", "ctx"), None),
            P(("groups", "ctx"), None),
            P(("groups", "ctx"), None),
            P(("groups", "ctx"), None),
            P(("groups", "ctx"), None),
            P("groups"),
            P("groups"),
        ),
        out_specs=(P(("groups", "ctx"), None), P(("groups", "ctx"), None)),
        check_vma=False,
    )
```

profile of v0, /device:TPU:0, one launch (start us, length us, event | category | flops | bytes accessed | tf_op | source)
XLA Modules:
  0.0 659.5 jit_solution(15291442228963987204)
XLA Ops:
  7.3 6.1 collective-permute-start
  13.3 2.5 collective-permute-start.1
  17.1 5.3 collective-permute-start.4
  22.3 2.6 collective-permute-start.5
  24.9 93.3 %all_gather.27 = bf16[256,1536]{1,0:T(8,128)(2,1)S(1)} all-gather(bf16[16,1536]{1,0:T(8,128)(2,1)} %param.17), channel_id=1, replica_groups=mesh['groups'=2,'ctx'=16] {'ctx'}, dimensions={0}, use_global_device_ids=true | all-gather | bytes 835584 | tf_op jit(solution)/shard_map/all_gather | solution.py:61
  118.2 24.4 %all_gather.28 = bf16[256,1536]{1,0:T(8,128)(2,1)} all-gather(bf16[16,1536]{1,0:T(8,128)(2,1)} %param.18), channel_id=1, replica_groups=mesh['groups'=2,'ctx'=16] {'ctx'}, dimensions={0}, use_global_device_ids=true | all-gather | bytes 835584 | tf_op jit(solution)/shard_map/all_gather | solution.py:62
  142.6 21.0 %all_gather.29 = bf16[256,1536]{1,0:T(8,128)(2,1)} all-gather(bf16[16,1536]{1,0:T(8,128)(2,1)S(1)} %copy-done.12), channel_id=1, replica_groups=mesh['groups'=2,'ctx'=16] {'ctx'}, dimensions={0}, use_global_device_ids=true | all-gather | bytes 835584 | tf_op jit(solution)/shard_map/all_gather | solution.py:60
  174.7 19.8 %collective-permute-done.3 = bf16[384,1536]{1,0:T(8,128)(2,1)S(1)} collective-permute-done((bf16[384,1536]{1,0:T(8,128)(2,1)S(1)}, bf16[384,1536]{1,0:T(8,128)(2,1)S(1)}, u32[]{:S(2)}, u32[]{:S(2)}) %collective-permute-start.3) | collective-permute-done | bytes 1179680 | tf_op jit(solution)/shard_map/ppermute | solution.py:16
  194.7 37.3 %collective-permute-done.7 = bf16[384,1536]{1,0:T(8,128)(2,1)S(1)} collective-permute-done((bf16[384,1536]{1,0:T(8,128)(2,1)}, bf16[384,1536]{1,0:T(8,128)(2,1)S(1)}, u32[]{:S(2)}, u32[]{:S(2)}) %collective-permute-start.7) | collective-permute-done | bytes 1179680 | tf_op jit(solution)/shard_map/ppermute | solution.py:16
  233.6 1.6 broadcast_in_dim.101
  235.4 179.9 %while.36 = (s32[]{:T(128)}, bf16[384,1536]{1,0:T(8,128)(2,1)}, f32[256,12]{0,1:T(8,128)S(1)}, f32[256,12]{0,1:T(8,128)S(1)}, f32[256,1536]{1,0:T(8,128)}, /*ind...) while((s32[]{:T(128)}, bf16[384,1536]{1,0:T(8,128)(2,1)}, ...), condition=%wide.region_10.11_spmd.clone.clone, body=%wide.region_1.10_spmd.clone.clone.sunk | while | flops 333393952 | bytes 24062668 | solution.py:174
  242.4 1.9 fusion.103
  248.2 1.9 fusion.109
  250.4 1.5 constant_dynamic-slice_fusion.11
  257.4 1.9 fusion.103
  263.1 1.9 fusion.109
  265.4 1.5 constant_dynamic-slice_fusion.11
  272.4 1.9 fusion.103
  278.1 1.9 fusion.109
  280.4 1.5 constant_dynamic-slice_fusion.11
  287.4 1.9 fusion.103
  293.1 1.9 fusion.109
  295.4 1.5 constant_dynamic-slice_fusion.11
  302.4 1.9 fusion.103
  308.1 1.8 fusion.109
  317.4 1.9 fusion.103
  323.1 1.8 fusion.109
  325.4 1.5 constant_dynamic-slice_fusion.11
  332.4 1.9 fusion.103
  338.1 1.8 fusion.109
  347.4 1.9 fusion.103
  353.1 1.9 fusion.109
  355.3 1.5 constant_dynamic-slice_fusion.11
  362.4 1.9 fusion.103
  368.1 1.9 fusion.109
  377.4 1.9 fusion.103
  383.1 1.9 fusion.109
  385.3 1.5 constant_dynamic-slice_fusion.11
  392.4 1.9 fusion.103
  398.1 1.9 fusion.109
  407.4 1.9 fusion.103
  413.1 1.9 fusion.109
  415.4 21.2 %all-gather = f32[4096,12]{0,1:T(8,128)S(1)} all-gather(f32[256,12]{0,1:T(8,128)S(1)} %get-tuple-element.794), channel_id=2, replica_groups=mesh['groups'=2,'ctx'=16] {'ctx'}, dimensions={0}, use_global_device_ids=true | all-gather | bytes 208896 | tf_op jit(solution)/shard_map/all_gather | solution.py:20
  436.6 19.5 %all-gather.1 = f32[4096,12]{0,1:T(8,128)S(1)} all-gather(f32[256,12]{0,1:T(8,128)S(1)} %get-tuple-element.795), channel_id=3, replica_groups=mesh['groups'=2,'ctx'=16] {'ctx'}, dimensions={0}, use_global_device_ids=true | all-gather | bytes 208896 | tf_op jit(solution)/shard_map/all_gather | solution.py:20
  456.2 90.8 %all-gather.5.cloned.1.call-done = f32[4096,1536]{1,0:T(8,128)} async-done(((f32[256,1536]{1,0:T(8,128)}), f32[4096,1536]{1,0:T(8,128)}) %all-gather.5.cloned.1.call-update) | async-done | bytes 25165840 | tf_op jit(solution)/shard_map/all_gather | solution.py:20
  548.4 1.6 copy.22
  550.0 16.3 %slice.39 = f32[3840,1536]{1,0:T(8,128)} slice(f32[4096,1536]{1,0:T(8,128)} %all-gather.5.cloned.1.call-done), slice={[256:4096], [0:1536]} | slice | bytes 47185920 | tf_op jit(solution)/shard_map/slice | solution.py:22
  566.3 83.5 %while.35 = (s32[]{:T(128)}, f32[256,12]{0,1:T(8,128)S(1)}, f32[256,12]{0,1:T(8,128)S(1)}, f32[256,1536]{0,1:T(8,128)}, f32[15,256,12]{1,0,2:T(8,128)S(1)}, /*in...) while((s32[]{:T(128)}, f32[256,12]{0,1:T(8,128)S(1)}, f32[256,12]{0,1:T(8,128)S(1)}, ...), condition=%wide.region_12.13_spmd, body=%wide.region_11.12_spmd.sunk | while | flops 1198082 | bytes 14131405 | solution.py:23
  569.1 2.8 fusion.87
  574.6 2.8 fusion.87
  580.2 2.8 fusion.87
  585.8 2.8 fusion.87
  591.4 2.8 fusion.87
  596.9 2.8 fusion.87
  602.5 2.8 fusion.87
  608.1 2.8 fusion.87
  613.6 2.8 fusion.87
  619.2 2.8 fusion.87
  624.8 2.8 fusion.87
  630.3 2.8 fusion.87
  635.9 2.8 fusion.87
  641.5 2.8 fusion.87
  647.0 2.8 fusion.87
  650.0 1.9 copy.26
  (578 shorter events, 179.5 us)
Async XLA Ops:
  7.2 156.7 %copy-start = (bf16[384,1536]{1,0:T(8,128)(2,1)S(1)}, bf16[384,1536]{1,0:T(8,128)(2,1)}, u32[]{:S(2)}) copy-start(bf16[384,1536]{1,0:T(8,128)(2,1)} %param.14) | copy-start | bytes 3538948
  7.2 135.4 %copy-start.12 = (bf16[16,1536]{1,0:T(8,128)(2,1)S(1)}, bf16[16,1536]{1,0:T(8,128)(2,1)}, u32[]{:S(2)}) copy-start(bf16[16,1536]{1,0:T(8,128)(2,1)} %param.16) | copy-start | bytes 147460
  7.2 156.4 %copy-start.13 = (s32[1,3]{1,0:T(1,128)S(1)}, s32[1,3]{1,0:T(1,128)}, u32[]{:S(2)}) copy-start(s32[1,3]{1,0:T(1,128)} %param.19) | copy-start | bytes 40
  7.2 156.4 %copy-start.14 = (s32[16]{0:T(128)S(1)}, s32[16]{0:T(128)}, u32[]{:S(2)}) copy-start(s32[16]{0:T(128)} %param.20) | copy-start | bytes 196
  7.2 539.8 %all-gather.5.cloned.1.call-start = ((), (), s32[]{:S(2)}) async-start(), calls=%async_computation | async-start | bytes 26738688 | tf_op jit(solution)/shard_map/all_gather | solution.py:20
  7.3 156.6 %collective-permute-start = (bf16[384,1536]{1,0:T(8,128)(2,1)}, bf16[384,1536]{1,0:T(8,128)(2,1)}, u32[]{:S(2)}, u32[]{:S(2)}) collective-permute-start(bf16[384,1536]{1,0:T(8,128)(2,1)} %param.14), channel_id=1, source_target_pairs={{0,2},{1,3},{2,4},{3,5},{4,6},{5,7},{6,8},{7,9},{8,10},{9,11},{10,... | collective-permute-start | bytes 3538952 | tf_op jit(solution)/shard_map/ppermute | solution.py:16
  13.3 153.2 %collective-permute-start.1 = (bf16[384,1536]{1,0:T(8,128)(2,1)}, bf16[384,1536]{1,0:T(8,128)(2,1)}, u32[]{:S(2)}, u32[]{:S(2)}) collective-permute-start(bf16[384,1536]{1,0:T(8,128)(2,1)} %param.14), channel_id=1, source_target_pairs={{0,1},{1,2},{2,3},{3,4},{4,5},{5,6},{6,7},{7,8},{8,9},{9,10},{10,1... | collective-permute-start | bytes 3538952 | tf_op jit(solution)/shard_map/ppermute | solution.py:16
  15.8 158.8 %collective-permute-start.2 = (bf16[384,1536]{1,0:T(8,128)(2,1)}, bf16[384,1536]{1,0:T(8,128)(2,1)S(1)}, u32[]{:S(2)}, u32[]{:S(2)}) collective-permute-start(bf16[384,1536]{1,0:T(8,128)(2,1)} %param.14), channel_id=1, source_target_pairs={{1,0},{2,1},{3,2},{4,3},{5,4},{6,5},{7,6},{8,7},{9,8},{10,9},{11,1... | collective-permute-start | bytes 3538952 | tf_op jit(solution)/shard_map/ppermute | solution.py:16
  17.1 152.2 %collective-permute-start.4 = (bf16[384,1536]{1,0:T(8,128)(2,1)}, bf16[384,1536]{1,0:T(8,128)(2,1)}, u32[]{:S(2)}, u32[]{:S(2)}) collective-permute-start(bf16[384,1536]{1,0:T(8,128)(2,1)} %param.15), channel_id=1, source_target_pairs={{0,2},{1,3},{2,4},{3,5},{4,6},{5,7},{6,8},{7,9},{8,10},{9,11},{10,... | collective-permute-start | bytes 3538952 | tf_op jit(solution)/shard_map/ppermute | solution.py:16
  22.3 149.6 %collective-permute-start.5 = (bf16[384,1536]{1,0:T(8,128)(2,1)}, bf16[384,1536]{1,0:T(8,128)(2,1)}, u32[]{:S(2)}, u32[]{:S(2)}) collective-permute-start(bf16[384,1536]{1,0:T(8,128)(2,1)} %param.15), channel_id=1, source_target_pairs={{0,1},{1,2},{2,3},{3,4},{4,5},{5,6},{6,7},{7,8},{8,9},{9,10},{10,1... | collective-permute-start | bytes 3538952 | tf_op jit(solution)/shard_map/ppermute | solution.py:16
  163.8 30.7 %collective-permute-start.3 = (bf16[384,1536]{1,0:T(8,128)(2,1)S(1)}, bf16[384,1536]{1,0:T(8,128)(2,1)S(1)}, u32[]{:S(2)}, u32[]{:S(2)}) collective-permute-start(bf16[384,1536]{1,0:T(8,128)(2,1)S(1)} %copy-done), channel_id=1, source_target_pairs={{2,0},{3,1},{4,2},{5,3},{6,4},{7,5},{8,6},{9,7},{10,8},{11,9},{12,... | collective-permute-start | bytes 3538952 | tf_op jit(solution)/shard_map/ppermute | solution.py:16
  166.5 28.1 %collective-permute-start.6 = (bf16[384,1536]{1,0:T(8,128)(2,1)}, bf16[384,1536]{1,0:T(8,128)(2,1)S(1)}, u32[]{:S(2)}, u32[]{:S(2)}) collective-permute-start(bf16[384,1536]{1,0:T(8,128)(2,1)} %param.15), channel_id=1, source_target_pairs={{1,0},{2,1},{3,2},{4,3},{5,4},{6,5},{7,6},{8,7},{9,8},{10,9},{11,1... | collective-permute-start | bytes 3538952 | tf_op jit(solution)/shard_map/ppermute | solution.py:16
  169.2 62.7 %collective-permute-start.7 = (bf16[384,1536]{1,0:T(8,128)(2,1)}, bf16[384,1536]{1,0:T(8,128)(2,1)S(1)}, u32[]{:S(2)}, u32[]{:S(2)}) collective-permute-start(bf16[384,1536]{1,0:T(8,128)(2,1)} %param.15), channel_id=1, source_target_pairs={{2,0},{3,1},{4,2},{5,3},{6,4},{7,5},{8,6},{9,7},{10,8},{11,9},{12,... | collective-permute-start | bytes 3538952 | tf_op jit(solution)/shard_map/ppermute | solution.py:16
  194.6 40.7 %copy-start.2 = (bf16[1920,1536]{1,0:T(8,128)(2,1)}, bf16[1920,1536]{1,0:T(8,128)(2,1)S(1)}, u32[]{:S(2)}) copy-start(bf16[1920,1536]{1,0:T(8,128)(2,1)S(1)} %constant_dynamic-update-slice_fusion) | copy-start | bytes 17694724
  232.1 3.4 copy-start.3
  235.4 4.3 copy-start.4
  242.4 7.9 %copy-start.1 = (bf16[384,1536]{1,0:T(8,128)(2,1)S(1)}, bf16[384,1536]{1,0:T(8,128)(2,1)}, u32[]{:S(2)}) copy-start(bf16[384,1536]{1,0:T(8,128)(2,1)} %get-tuple-element.814) | copy-start | bytes 3538948 | tf_op jit(solution)/shard_map/while
  242.4 7.9 %copy-start.5 = (bf16[256,1536]{1,0:T(8,128)(2,1)S(1)}, bf16[256,1536]{1,0:T(8,128)(2,1)}, u32[]{:S(2)}) copy-start(bf16[256,1536]{1,0:T(8,128)(2,1)} %copy-done.4) | copy-start | bytes 2359300 | tf_op jit(solution)/shard_map/while
  250.4 4.3 copy-start.4
  257.4 8.0 %copy-start.1 = (bf16[384,1536]{1,0:T(8,128)(2,1)S(1)}, bf16[384,1536]{1,0:T(8,128)(2,1)}, u32[]{:S(2)}) copy-start(bf16[384,1536]{1,0:T(8,128)(2,1)} %get-tuple-element.814) | copy-start | bytes 3538948 | tf_op jit(solution)/shard_map/while
  257.4 8.0 %copy-start.5 = (bf16[256,1536]{1,0:T(8,128)(2,1)S(1)}, bf16[256,1536]{1,0:T(8,128)(2,1)}, u32[]{:S(2)}) copy-start(bf16[256,1536]{1,0:T(8,128)(2,1)} %copy-done.4) | copy-start | bytes 2359300 | tf_op jit(solution)/shard_map/while
  265.4 4.3 copy-start.4
  272.4 8.0 %copy-start.1 = (bf16[384,1536]{1,0:T(8,128)(2,1)S(1)}, bf16[384,1536]{1,0:T(8,128)(2,1)}, u32[]{:S(2)}) copy-start(bf16[384,1536]{1,0:T(8,128)(2,1)} %get-tuple-element.814) | copy-start | bytes 3538948 | tf_op jit(solution)/shard_map/while
  272.4 8.0 %copy-start.5 = (bf16[256,1536]{1,0:T(8,128)(2,1)S(1)}, bf16[256,1536]{1,0:T(8,128)(2,1)}, u32[]{:S(2)}) copy-start(bf16[256,1536]{1,0:T(8,128)(2,1)} %copy-done.4) | copy-start | bytes 2359300 | tf_op jit(solution)/shard_map/while
  280.4 4.3 copy-start.4
  287.4 7.9 %copy-start.1 = (bf16[384,1536]{1,0:T(8,128)(2,1)S(1)}, bf16[384,1536]{1,0:T(8,128)(2,1)}, u32[]{:S(2)}) copy-start(bf16[384,1536]{1,0:T(8,128)(2,1)} %get-tuple-element.814) | copy-start | bytes 3538948 | tf_op jit(solution)/shard_map/while
  287.4 7.9 %copy-start.5 = (bf16[256,1536]{1,0:T(8,128)(2,1)S(1)}, bf16[256,1536]{1,0:T(8,128)(2,1)}, u32[]{:S(2)}) copy-start(bf16[256,1536]{1,0:T(8,128)(2,1)} %copy-done.4) | copy-start | bytes 2359300 | tf_op jit(solution)/shard_map/while
  295.4 4.3 copy-start.4
  302.4 7.9 %copy-start.1 = (bf16[384,1536]{1,0:T(8,128)(2,1)S(1)}, bf16[384,1536]{1,0:T(8,128)(2,1)}, u32[]{:S(2)}) copy-start(bf16[384,1536]{1,0:T(8,128)(2,1)} %get-tuple-element.814) | copy-start | bytes 3538948 | tf_op jit(solution)/shard_map/while
  302.4 7.9 %copy-start.5 = (bf16[256,1536]{1,0:T(8,128)(2,1)S(1)}, bf16[256,1536]{1,0:T(8,128)(2,1)}, u32[]{:S(2)}) copy-start(bf16[256,1536]{1,0:T(8,128)(2,1)} %copy-done.4) | copy-start | bytes 2359300 | tf_op jit(solution)/shard_map/while
  310.4 4.3 copy-start.4
  317.4 7.9 %copy-start.1 = (bf16[384,1536]{1,0:T(8,128)(2,1)S(1)}, bf16[384,1536]{1,0:T(8,128)(2,1)}, u32[]{:S(2)}) copy-start(bf16[384,1536]{1,0:T(8,128)(2,1)} %get-tuple-element.814) | copy-start | bytes 3538948 | tf_op jit(solution)/shard_map/while
  317.4 7.9 %copy-start.5 = (bf16[256,1536]{1,0:T(8,128)(2,1)S(1)}, bf16[256,1536]{1,0:T(8,128)(2,1)}, u32[]{:S(2)}) copy-start(bf16[256,1536]{1,0:T(8,128)(2,1)} %copy-done.4) | copy-start | bytes 2359300 | tf_op jit(solution)/shard_map/while
  325.3 4.3 copy-start.4
  332.4 7.9 %copy-start.1 = (bf16[384,1536]{1,0:T(8,128)(2,1)S(1)}, bf16[384,1536]{1,0:T(8,128)(2,1)}, u32[]{:S(2)}) copy-start(bf16[384,1536]{1,0:T(8,128)(2,1)} %get-tuple-element.814) | copy-start | bytes 3538948 | tf_op jit(solution)/shard_map/while
  332.4 7.9 %copy-start.5 = (bf16[256,1536]{1,0:T(8,128)(2,1)S(1)}, bf16[256,1536]{1,0:T(8,128)(2,1)}, u32[]{:S(2)}) copy-start(bf16[256,1536]{1,0:T(8,128)(2,1)} %copy-done.4) | copy-start | bytes 2359300 | tf_op jit(solution)/shard_map/while
  340.3 4.3 copy-start.4
  347.3 8.0 %copy-start.1 = (bf16[384,1536]{1,0:T(8,128)(2,1)S(1)}, bf16[384,1536]{1,0:T(8,128)(2,1)}, u32[]{:S(2)}) copy-start(bf16[384,1536]{1,0:T(8,128)(2,1)} %get-tuple-element.814) | copy-start | bytes 3538948 | tf_op jit(solution)/shard_map/while
  347.3 8.0 %copy-start.5 = (bf16[256,1536]{1,0:T(8,128)(2,1)S(1)}, bf16[256,1536]{1,0:T(8,128)(2,1)}, u32[]{:S(2)}) copy-start(bf16[256,1536]{1,0:T(8,128)(2,1)} %copy-done.4) | copy-start | bytes 2359300 | tf_op jit(solution)/shard_map/while
  355.3 4.3 copy-start.4
  362.3 8.0 %copy-start.1 = (bf16[384,1536]{1,0:T(8,128)(2,1)S(1)}, bf16[384,1536]{1,0:T(8,128)(2,1)}, u32[]{:S(2)}) copy-start(bf16[384,1536]{1,0:T(8,128)(2,1)} %get-tuple-element.814) | copy-start | bytes 3538948 | tf_op jit(solution)/shard_map/while
  362.4 8.0 %copy-start.5 = (bf16[256,1536]{1,0:T(8,128)(2,1)S(1)}, bf16[256,1536]{1,0:T(8,128)(2,1)}, u32[]{:S(2)}) copy-start(bf16[256,1536]{1,0:T(8,128)(2,1)} %copy-done.4) | copy-start | bytes 2359300 | tf_op jit(solution)/shard_map/while
  370.3 4.3 copy-start.4
  377.3 8.0 %copy-start.1 = (bf16[384,1536]{1,0:T(8,128)(2,1)S(1)}, bf16[384,1536]{1,0:T(8,128)(2,1)}, u32[]{:S(2)}) copy-start(bf16[384,1536]{1,0:T(8,128)(2,1)} %get-tuple-element.814) | copy-start | bytes 3538948 | tf_op jit(solution)/shard_map/while
  377.4 8.0 %copy-start.5 = (bf16[256,1536]{1,0:T(8,128)(2,1)S(1)}, bf16[256,1536]{1,0:T(8,128)(2,1)}, u32[]{:S(2)}) copy-start(bf16[256,1536]{1,0:T(8,128)(2,1)} %copy-done.4) | copy-start | bytes 2359300 | tf_op jit(solution)/shard_map/while
  385.3 4.3 copy-start.4
  392.3 8.0 %copy-start.1 = (bf16[384,1536]{1,0:T(8,128)(2,1)S(1)}, bf16[384,1536]{1,0:T(8,128)(2,1)}, u32[]{:S(2)}) copy-start(bf16[384,1536]{1,0:T(8,128)(2,1)} %get-tuple-element.814) | copy-start | bytes 3538948 | tf_op jit(solution)/shard_map/while
  392.4 8.0 %copy-start.5 = (bf16[256,1536]{1,0:T(8,128)(2,1)S(1)}, bf16[256,1536]{1,0:T(8,128)(2,1)}, u32[]{:S(2)}) copy-start(bf16[256,1536]{1,0:T(8,128)(2,1)} %copy-done.4) | copy-start | bytes 2359300 | tf_op jit(solution)/shard_map/while
  400.3 4.3 copy-start.4
  407.4 8.0 %copy-start.1 = (bf16[384,1536]{1,0:T(8,128)(2,1)S(1)}, bf16[384,1536]{1,0:T(8,128)(2,1)}, u32[]{:S(2)}) copy-start(bf16[384,1536]{1,0:T(8,128)(2,1)} %get-tuple-element.814) | copy-start | bytes 3538948 | tf_op jit(solution)/shard_map/while
  407.4 8.0 %copy-start.5 = (bf16[256,1536]{1,0:T(8,128)(2,1)S(1)}, bf16[256,1536]{1,0:T(8,128)(2,1)}, u32[]{:S(2)}) copy-start(bf16[256,1536]{1,0:T(8,128)(2,1)} %copy-done.4) | copy-start | bytes 2359300 | tf_op jit(solution)/shard_map/while
  436.6 110.4 %copy-start.6 = (f32[4096,12]{0,1:T(8,128)}, f32[4096,12]{0,1:T(8,128)S(1)}, u32[]{:S(2)}) copy-start(f32[4096,12]{0,1:T(8,128)S(1)} %all-gather) | copy-start | bytes 589828
  456.1 91.0 %copy-start.7 = (f32[4096,12]{0,1:T(8,128)}, f32[4096,12]{0,1:T(8,128)S(1)}, u32[]{:S(2)}) copy-start(f32[4096,12]{0,1:T(8,128)S(1)} %all-gather.1) | copy-start | bytes 589828
  550.0 16.3 %slice-start.1 = ((f32[4096,12]{0,1:T(8,128)}), f32[256,12]{0,1:T(8,128)S(1)}, s32[]{:S(2)}) async-start(f32[4096,12]{0,1:T(8,128)} %copy-done.6), calls=%async_computation.2 | async-start | bytes 32768 | tf_op jit(solution)/shard_map/slice | solution.py:21
  550.0 16.3 %slice-start.2 = ((f32[4096,12]{0,1:T(8,128)}), f32[256,12]{0,1:T(8,128)S(1)}, s32[]{:S(2)}) async-start(f32[4096,12]{0,1:T(8,128)} %copy-done.7), calls=%async_computation.3 | async-start | bytes 32768 | tf_op jit(solution)/shard_map/slice | solution.py:21
  569.1 2.8 copy-start.9
  574.6 2.8 copy-start.9
  585.8 2.8 copy-start.9
  596.9 2.8 copy-start.9
  602.5 2.8 copy-start.9
  613.6 2.8 copy-start.9
  619.2 2.8 copy-start.9
  630.3 2.8 copy-start.9
  647.0 2.8 copy-start.9
  (52 other events, 82.2 us)
Sparse Core Ops, SparseCore 0:
  415.5 131.4 all-gather.4
where the time goes:
time: 664 us; the launch traced here: 660 us
  blocking collectives  179 us (27%)
  waiting for transfers between devices  148 us (22%)
  matrix products  119 us (18%)
  local copies, waits for them, and re-layouts  107 us (16%)
  other arithmetic  68.2 us (10%)
  starting transfers between devices  21.5 us (3%)
  between operations  14.3 us (2%)
    all_gather x1, blocking collectives, on_device(): lax.all_gather(key_text, 'ctx', axis=0, tiled=True)  93.3 us
    all_gather x1, waiting for transfers between devices, combined_all(): pieces = jax.tree.map(lambda part: lax.all_gather(part, axis), value)  90.8 us
    ppermute x8, waiting for transfers between devices, shifted(): return lax.ppermute(shard, axis, pairs)  57.1 us
    add x15, other arithmetic, combine_parts(): acc_early * spread_heads(factor_early)  42.2 us
    all_gather x2, blocking collectives, combined_all(): pieces = jax.tree.map(lambda part: lax.all_gather(part, axis), value)  40.7 us
    dynamic_slice x45, local copies, waits for them, and re-layouts, combined_all(): lax.scan(lambda total, share: (join(total, share), None), head, tail)  30.1 us
    all_gather x1, blocking collectives, on_device(): lax.all_gather(value_text, 'ctx', axis=0, tiled=True)  24.4 us
    dot_general x12, matrix products, head_step(): jnp.einsum('tqk,kd->tqd', weight_text.astype(jnp.bfloat16), value_words,...  22.7 us
  transfers between devices with their start and end apart: 9, of which 3 were waited for; matrix products, arithmetic and copies ran while one was open for 1% of the time, Pallas kernels for 0%

commit v1 on v0

--- a/solution.py
+++ b/solution.py
@@ -3,11 +3,42 @@
 import jax.numpy as jnp
 from jax import lax
 from jax.sharding import PartitionSpec as P
+from jax.lax import axis_index, axis_size, ppermute
 
 TILE = 384
 HD = 128
 NB = 3
 REACH = 2
+
+
+def mark_spots(message):
+    ax_name = "ctx"
+    seen_now = axis_size(ax_name)
+    parts_out, p_next, low = (seen_now, axis_index(ax_name), message.shape[0])
+    frames = []
+    for j0, kk in enumerate(message.shape):
+        frames.append(kk * parts_out if j0 == 0 else kk)
+    latest = lax.dynamic_update_slice_in_dim(
+        jnp.zeros(frames, message.dtype), message, p_next * low, axis=0
+    )
+    x_now = reply = message
+    for t in [*range(1, parts_out // 2 + 1)]:
+        shelf = []
+        for j0 in [*range(parts_out)]:
+            shelf.append((j0, (j0 + 1) % parts_out))
+        x_now = ppermute(x_now, ax_name, shelf)
+        latest = lax.dynamic_update_slice_in_dim(
+            latest, x_now, (p_next - t) % parts_out * low, axis=0
+        )
+        if 2 * t < parts_out:
+            log = []
+            for j0 in tuple(range(parts_out)):
+                log.append((j0, (j0 - 1) % parts_out))
+            reply = ppermute(reply, ax_name, log)
+            latest = lax.dynamic_update_slice_in_dim(
+                latest, reply, (p_next + t) % parts_out * low, axis=0
+            )
+    return latest
 
 
 def shifted(shard, axis, by):
@@ -59,7 +90,7 @@
     text_query, text_keys, text_values = (
         lax.all_gather(query_text, "ctx", axis=0, tiled=True),
         lax.all_gather(key_text, "ctx", axis=0, tiled=True),
-        lax.all_gather(value_text, "ctx", axis=0, tiled=True),
+        mark_spots(value_text),
     )
     text_rows = text_keys.shape[0]
     text_limit = text_count[0]

time: 664 us -> 687 us (1.035)
  waiting for transfers between devices: 148 us -> 208 us
  blocking collectives: 179 us -> 140 us
  matrix products: 119 us -> 111 us
  local copies, waits for them, and re-layouts: 107 us -> 115 us
    ppermute x0 -> x15, waiting for transfers between devices: none -> 60.4 us  [the longest x8 34.7 us: mark_spots(): x_now = ppermute(x_now, ax_name, shelf)]
    all_gather x1, blocking collectives: 93.3 us -> 63.2 us  [on_device(): lax.all_gather(key_text, 'ctx', axis=0, tiled=True)]
    all_gather x1 -> x0, blocking collectives: 24.4 us -> none  [on_device(): lax.all_gather(value_text, 'ctx', axis=0, tiled=True)]
    all_gather x2, blocking collectives: 40.7 us -> 52.1 us  [combined_all(): pieces = jax.tree.map(lambda part: lax.all_gather(part, axis), value)]
    ppermute x0 -> x15, starting transfers between devices: none -> 10.2 us  [the longest x8 5.16 us: mark_spots(): x_now = ppermute(x_now, ax_name, shelf)]
    dynamic_update_slice x0 -> x16, local copies, waits for them, and re-layouts: none -> 9.9 us  [the longest x8 4.96 us: mark_spots(): lax.dynamic_update_slice_in_dim(latest, x_now, (p_next - t) % parts_out *...]
    ppermute x8, starting transfers between devices: 21.5 us -> 12.5 us  [shifted(): return lax.ppermute(shard, axis, pairs)]
    dot_general x12, matrix products: 10.8 us -> 2.54 us  [head_step(): jnp.einsum('tk,kd->td', weight_own.astype(jnp.bfloat16), value_own_text,...]
  transfers between devices with their start and end apart: 9 -> 24, of which waited for: 3 -> 16; matrix products, arithmetic and copies ran while one was open for 1% -> 2% of each run, Pallas kernels for 0% -> 0%
where the time goes in v1:
time: 687 us; the launch traced here: 682 us
  waiting for transfers between devices  208 us (30%)
  blocking collectives  140 us (20%)
  local copies, waits for them, and re-layouts  115 us (17%)
  matrix products  111 us (16%)
  other arithmetic  68.7 us (10%)
  starting transfers between devices  22.8 us (3%)
  between operations  14.7 us (2%)
    all_gather x1, waiting for transfers between devices, combined_all(): pieces = jax.tree.map(lambda part: lax.all_gather(part, axis), value)  90.8 us
    all_gather x1, blocking collectives, on_device(): lax.all_gather(key_text, 'ctx', axis=0, tiled=True)  63.2 us
    ppermute x8, waiting for transfers between devices, shifted(): return lax.ppermute(shard, axis, pairs)  56.6 us
    all_gather x2, blocking collectives, combined_all(): pieces = jax.tree.map(lambda part: lax.all_gather(part, axis), value)  52.1 us
    add x15, other arithmetic, combine_parts(): acc_early * spread_heads(factor_early)  42.7 us
    ppermute x8, waiting for transfers between devices, mark_spots(): x_now = ppermute(x_now, ax_name, shelf)  34.7 us
    dynamic_slice x45, local copies, waits for them, and re-layouts, combined_all(): lax.scan(lambda total, share: (join(total, share), None), head, tail)  30.1 us
    ppermute x7, waiting for transfers between devices, mark_spots(): reply = ppermute(reply, ax_name, log)  25.8 us
  transfers between devices with their start and end apart: 24, of which 16 were waited for; matrix products, arithmetic and copies ran while one was open for 2% of the time, Pallas kernels for 0%

profile of v1, /device:TPU:0, one launch (start us, length us, event | category | flops | bytes accessed | tf_op | source)
XLA Modules:
  0.0 682.3 jit_solution(15692837529928406859)
XLA Ops:
  7.7 5.1 collective-permute-start.9
  12.8 2.3 collective-permute-start
  15.1 2.4 collective-permute-start.1
  18.8 63.2 %all_gather.24 = bf16[256,1536]{1,0:T(8,128)(2,1)S(1)} all-gather(bf16[16,1536]{1,0:T(8,128)(2,1)} %param.17), channel_id=1, replica_groups=mesh['groups'=2,'ctx'=16] {'ctx'}, dimensions={0}, use_global_device_ids=true | all-gather | bytes 835584 | tf_op jit(solution)/shard_map/all_gather | solution.py:92
  82.0 24.4 %all_gather.25 = bf16[256,1536]{1,0:T(8,128)(2,1)} all-gather(bf16[16,1536]{1,0:T(8,128)(2,1)} %param.16), channel_id=1, replica_groups=mesh['groups'=2,'ctx'=16] {'ctx'}, dimensions={0}, use_global_device_ids=true | all-gather | bytes 835584 | tf_op jit(solution)/shard_map/all_gather | solution.py:91
  111.5 5.3 collective-permute-done.10
  117.4 20.1 %collective-permute-done.11 = bf16[16,1536]{1,0:T(8,128)(2,1)S(1)} collective-permute-done((bf16[16,1536]{1,0:T(8,128)(2,1)S(1)}, bf16[16,1536]{1,0:T(8,128)(2,1)S(1)}, u32[]{:S(2)}, u32[]{:S(2)}) %collective-permute-start.11) | collective-permute-done | bytes 49184 | tf_op jit(solution)/shard_map/ppermute | solution.py:37
  137.5 3.5 collective-permute-start.12
  141.6 2.1 collective-permute-done.12
  146.9 4.9 collective-permute-done.14
  154.1 5.6 collective-permute-done.16
  162.1 5.6 collective-permute-done.18
  170.1 5.6 collective-permute-done.20
  178.1 5.6 collective-permute-done.22
  194.0 22.5 %collective-permute-done.3 = bf16[384,1536]{1,0:T(8,128)(2,1)S(1)} collective-permute-done((bf16[384,1536]{1,0:T(8,128)(2,1)S(1)}, bf16[384,1536]{1,0:T(8,128)(2,1)S(1)}, u32[]{:S(2)}, u32[]{:S(2)}) %collective-permute-start.3) | collective-permute-done | bytes 1179680 | tf_op jit(solution)/shard_map/ppermute | solution.py:47
  216.6 34.1 %collective-permute-done.7 = bf16[384,1536]{1,0:T(8,128)(2,1)S(1)} collective-permute-done((bf16[384,1536]{1,0:T(8,128)(2,1)}, bf16[384,1536]{1,0:T(8,128)(2,1)S(1)}, u32[]{:S(2)}, u32[]{:S(2)}) %collective-permute-start.7) | collective-permute-done | bytes 1179680 | tf_op jit(solution)/shard_map/ppermute | solution.py:47
  252.4 1.6 broadcast_in_dim.104
  254.2 171.7 %while.36 = (s32[]{:T(128)}, bf16[384,1536]{1,0:T(8,128)(2,1)}, f32[256,12]{0,1:T(8,128)S(1)}, f32[256,12]{0,1:T(8,128)S(1)}, f32[256,1536]{1,0:T(8,128)}, /*ind...) while((s32[]{:T(128)}, bf16[384,1536]{1,0:T(8,128)(2,1)}, ...), condition=%wide.region_10.11_spmd.clone.clone, body=%wide.region_1.10_spmd.clone.clone.sunk | while | flops 333393952 | bytes 24062668 | solution.py:205
  261.2 1.9 fusion.103
  266.3 1.8 fusion.109
  275.5 1.9 fusion.103
  280.6 1.9 fusion.109
  289.8 1.9 fusion.103
  294.9 1.9 fusion.109
  304.2 1.9 fusion.103
  309.2 1.9 fusion.109
  318.5 1.9 fusion.103
  323.5 1.9 fusion.109
  332.8 1.9 fusion.103
  337.8 1.8 fusion.109
  347.1 1.9 fusion.103
  352.1 1.9 fusion.109
  361.4 1.9 fusion.103
  366.4 1.9 fusion.109
  375.7 1.9 fusion.103
  380.7 1.9 fusion.109
  390.0 1.9 fusion.103
  395.0 1.8 fusion.109
  404.3 1.9 fusion.103
  409.3 1.9 fusion.109
  418.6 1.9 fusion.103
  423.7 1.9 fusion.109
  425.9 32.6 %all-gather = f32[4096,12]{0,1:T(8,128)S(1)} all-gather(f32[256,12]{0,1:T(8,128)S(1)} %get-tuple-element.794), channel_id=2, replica_groups=mesh['groups'=2,'ctx'=16] {'ctx'}, dimensions={0}, use_global_device_ids=true | all-gather | bytes 208896 | tf_op jit(solution)/shard_map/all_gather | solution.py:51
  458.6 19.5 %all-gather.1 = f32[4096,12]{0,1:T(8,128)S(1)} all-gather(f32[256,12]{0,1:T(8,128)S(1)} %get-tuple-element.795), channel_id=3, replica_groups=mesh['groups'=2,'ctx'=16] {'ctx'}, dimensions={0}, use_global_device_ids=true | all-gather | bytes 208896 | tf_op jit(solution)/shard_map/all_gather | solution.py:51
  478.2 90.8 %all-gather.5.cloned.1.call-done = f32[4096,1536]{1,0:T(8,128)} async-done(((f32[256,1536]{1,0:T(8,128)}), f32[4096,1536]{1,0:T(8,128)}) %all-gather.5.cloned.1.call-update) | async-done | bytes 25165840 | tf_op jit(solution)/shard_map/all_gather | solution.py:51
  570.4 1.6 copy.22
  572.0 16.3 %slice.39 = f32[3840,1536]{1,0:T(8,128)} slice(f32[4096,1536]{1,0:T(8,128)} %all-gather.5.cloned.1.call-done), slice={[256:4096], [0:1536]} | slice | bytes 47185920 | tf_op jit(solution)/shard_map/slice | solution.py:53
  588.3 84.3 %while.35 = (s32[]{:T(128)}, f32[256,12]{0,1:T(8,128)S(1)}, f32[256,12]{0,1:T(8,128)S(1)}, f32[256,1536]{0,1:T(8,128)}, f32[15,256,12]{1,0,2:T(8,128)S(1)}, /*in...) while((s32[]{:T(128)}, f32[256,12]{0,1:T(8,128)S(1)}, f32[256,12]{0,1:T(8,128)S(1)}, ...), condition=%wide.region_12.13_spmd, body=%wide.region_11.12_spmd.sunk | while | flops 1198082 | bytes 14131405 | solution.py:54
  591.1 2.8 fusion.87
  596.7 2.8 fusion.87
  602.3 2.8 fusion.87
  607.9 2.8 fusion.87
  613.6 2.8 fusion.87
  619.2 2.8 fusion.87
  624.8 2.8 fusion.87
  630.4 2.8 fusion.87
  636.0 2.8 fusion.87
  641.6 2.8 fusion.87
  647.3 2.8 fusion.87
  652.9 2.8 fusion.87
  658.5 2.8 fusion.87
  664.1 2.8 fusion.87
  669.7 2.8 fusion.87
  672.6 1.9 copy.26
  (624 shorter events, 200.6 us)
Async XLA Ops:
  7.2 100.2 %copy-start.12 = (bf16[16,1536]{1,0:T(8,128)(2,1)S(1)}, bf16[16,1536]{1,0:T(8,128)(2,1)}, u32[]{:S(2)}) copy-start(bf16[16,1536]{1,0:T(8,128)(2,1)} %param.18) | copy-start | bytes 147460
  7.2 100.8 %copy-start.13 = (s32[1,3]{1,0:T(1,128)S(1)}, s32[1,3]{1,0:T(1,128)}, u32[]{:S(2)}) copy-start(s32[1,3]{1,0:T(1,128)} %param.19) | copy-start | bytes 40
  7.2 100.8 %copy-start.14 = (s32[16]{0:T(128)S(1)}, s32[16]{0:T(128)}, u32[]{:S(2)}) copy-start(s32[16]{0:T(128)} %param.20) | copy-start | bytes 196
  7.2 561.8 %all-gather.5.cloned.1.call-start = ((), (), s32[]{:S(2)}) async-start(), calls=%async_computation | async-start | bytes 26738688 | tf_op jit(solution)/shard_map/all_gather | solution.py:51
  7.2 101.3 %collective-permute-start.8 = (bf16[16,1536]{1,0:T(8,128)(2,1)}, bf16[16,1536]{1,0:T(8,128)(2,1)S(1)}, u32[]{:S(2)}, u32[]{:S(2)}) collective-permute-start(bf16[16,1536]{1,0:T(8,128)(2,1)} %param.18), channel_id=1, source_target_pairs={{0,1},{1,2},{2,3},{3,4},{4,5},{5,6},{6,7},{7,8},{8,9},{9,10},{10,1... | collective-permute-start | bytes 147464 | tf_op jit(solution)/shard_map/ppermute | solution.py:29
  7.7 102.8 %collective-permute-start.9 = (bf16[16,1536]{1,0:T(8,128)(2,1)}, bf16[16,1536]{1,0:T(8,128)(2,1)S(1)}, u32[]{:S(2)}, u32[]{:S(2)}) collective-permute-start(bf16[16,1536]{1,0:T(8,128)(2,1)} %param.18), channel_id=1, source_target_pairs={{0,15},{1,0},{2,1},{3,2},{4,3},{5,4},{6,5},{7,6},{8,7},{9,8},{10,9... | collective-permute-start | bytes 147464 | tf_op jit(solution)/shard_map/ppermute | solution.py:37
  12.8 172.9 %collective-permute-start = (bf16[384,1536]{1,0:T(8,128)(2,1)}, bf16[384,1536]{1,0:T(8,128)(2,1)}, u32[]{:S(2)}, u32[]{:S(2)}) collective-permute-start(bf16[384,1536]{1,0:T(8,128)(2,1)} %param.14), channel_id=1, source_target_pairs={{0,2},{1,3},{2,4},{3,5},{4,6},{5,7},{6,8},{7,9},{8,10},{9,11},{10,... | collective-permute-start | bytes 3538952 | tf_op jit(solution)/shard_map/ppermute | solution.py:47
  15.1 173.2 %collective-permute-start.1 = (bf16[384,1536]{1,0:T(8,128)(2,1)}, bf16[384,1536]{1,0:T(8,128)(2,1)}, u32[]{:S(2)}, u32[]{:S(2)}) collective-permute-start(bf16[384,1536]{1,0:T(8,128)(2,1)} %param.14), channel_id=1, source_target_pairs={{0,1},{1,2},{2,3},{3,4},{4,5},{5,6},{6,7},{7,8},{8,9},{9,10},{10,1... | collective-permute-start | bytes 3538952 | tf_op jit(solution)/shard_map/ppermute | solution.py:47
  17.5 176.4 %collective-permute-start.2 = (bf16[384,1536]{1,0:T(8,128)(2,1)}, bf16[384,1536]{1,0:T(8,128)(2,1)S(1)}, u32[]{:S(2)}, u32[]{:S(2)}) collective-permute-start(bf16[384,1536]{1,0:T(8,128)(2,1)} %param.14), channel_id=1, source_target_pairs={{1,0},{2,1},{3,2},{4,3},{5,4},{6,5},{7,6},{8,7},{9,8},{10,9},{11,1... | collective-permute-start | bytes 3538952 | tf_op jit(solution)/shard_map/ppermute | solution.py:47
  106.4 79.3 %copy-start = (bf16[384,1536]{1,0:T(8,128)(2,1)S(1)}, bf16[384,1536]{1,0:T(8,128)(2,1)}, u32[]{:S(2)}) copy-start(bf16[384,1536]{1,0:T(8,128)(2,1)} %param.14) | copy-start | bytes 3538948
  108.5 82.5 %collective-permute-start.4 = (bf16[384,1536]{1,0:T(8,128)(2,1)}, bf16[384,1536]{1,0:T(8,128)(2,1)S(1)}, u32[]{:S(2)}, u32[]{:S(2)}) collective-permute-start(bf16[384,1536]{1,0:T(8,128)(2,1)} %param.15), channel_id=1, source_target_pairs={{0,2},{1,3},{2,4},{3,5},{4,6},{5,7},{6,8},{7,9},{8,10},{9,11},{10,... | collective-permute-start | bytes 3538952 | tf_op jit(solution)/shard_map/ppermute | solution.py:47
  110.5 6.2 collective-permute-start.10
  116.8 20.7 %collective-permute-start.11 = (bf16[16,1536]{1,0:T(8,128)(2,1)S(1)}, bf16[16,1536]{1,0:T(8,128)(2,1)S(1)}, u32[]{:S(2)}, u32[]{:S(2)}) collective-permute-start(bf16[16,1536]{1,0:T(8,128)(2,1)S(1)} %collective-permute-done.9), channel_id=1, source_target_pairs={{0,15},{1,0},{2,1},{3,2},{4,3},{5,4},{6,5},{7,6},{8,7},{9,8},{10,9... | collective-permute-start | bytes 147464 | tf_op jit(solution)/shard_map/ppermute | solution.py:37
  137.5 6.2 collective-permute-start.12
  143.7 1.8 collective-permute-start.13
  145.4 6.3 collective-permute-start.14
  151.7 1.8 collective-permute-start.15
  153.5 6.2 collective-permute-start.16
  159.7 1.8 collective-permute-start.17
  161.5 6.2 collective-permute-start.18
  167.7 1.8 collective-permute-start.19
  169.4 6.2 collective-permute-start.20
  175.7 1.8 collective-permute-start.21
  177.4 6.2 collective-permute-start.22
  183.7 8.8 %collective-permute-start.5 = (bf16[384,1536]{1,0:T(8,128)(2,1)}, bf16[384,1536]{1,0:T(8,128)(2,1)S(1)}, u32[]{:S(2)}, u32[]{:S(2)}) collective-permute-start(bf16[384,1536]{1,0:T(8,128)(2,1)} %param.15), channel_id=1, source_target_pairs={{0,1},{1,2},{2,3},{3,4},{4,5},{5,6},{6,7},{7,8},{8,9},{9,10},{10,1... | collective-permute-start | bytes 3538952 | tf_op jit(solution)/shard_map/ppermute | solution.py:47
  185.7 30.8 %collective-permute-start.3 = (bf16[384,1536]{1,0:T(8,128)(2,1)S(1)}, bf16[384,1536]{1,0:T(8,128)(2,1)S(1)}, u32[]{:S(2)}, u32[]{:S(2)}) collective-permute-start(bf16[384,1536]{1,0:T(8,128)(2,1)S(1)} %copy-done), channel_id=1, source_target_pairs={{2,0},{3,1},{4,2},{5,3},{6,4},{7,5},{8,6},{9,7},{10,8},{11,9},{12,... | collective-permute-start | bytes 3538952 | tf_op jit(solution)/shard_map/ppermute | solution.py:47
  188.3 28.2 %collective-permute-start.6 = (bf16[384,1536]{1,0:T(8,128)(2,1)}, bf16[384,1536]{1,0:T(8,128)(2,1)S(1)}, u32[]{:S(2)}, u32[]{:S(2)}) collective-permute-start(bf16[384,1536]{1,0:T(8,128)(2,1)} %param.15), channel_id=1, source_target_pairs={{1,0},{2,1},{3,2},{4,3},{5,4},{6,5},{7,6},{8,7},{9,8},{10,9},{11,1... | collective-permute-start | bytes 3538952 | tf_op jit(solution)/shard_map/ppermute | solution.py:47
  191.1 59.7 %collective-permute-start.7 = (bf16[384,1536]{1,0:T(8,128)(2,1)}, bf16[384,1536]{1,0:T(8,128)(2,1)S(1)}, u32[]{:S(2)}, u32[]{:S(2)}) collective-permute-start(bf16[384,1536]{1,0:T(8,128)(2,1)} %param.15), channel_id=1, source_target_pairs={{2,0},{3,1},{4,2},{5,3},{6,4},{7,5},{8,6},{9,7},{10,8},{11,9},{12,... | collective-permute-start | bytes 3538952 | tf_op jit(solution)/shard_map/ppermute | solution.py:47
  216.5 37.5 %copy-start.2 = (bf16[1920,1536]{1,0:T(8,128)(2,1)}, bf16[1920,1536]{1,0:T(8,128)(2,1)S(1)}, u32[]{:S(2)}) copy-start(bf16[1920,1536]{1,0:T(8,128)(2,1)S(1)} %constant_dynamic-update-slice_fusion) | copy-start | bytes 17694724
  261.2 7.2 %copy-start.1 = (bf16[384,1536]{1,0:T(8,128)(2,1)S(1)}, bf16[384,1536]{1,0:T(8,128)(2,1)}, u32[]{:S(2)}) copy-start(bf16[384,1536]{1,0:T(8,128)(2,1)} %get-tuple-element.814) | copy-start | bytes 3538948 | tf_op jit(solution)/shard_map/while
  261.2 7.2 %copy-start.5 = (bf16[256,1536]{1,0:T(8,128)(2,1)S(1)}, bf16[256,1536]{1,0:T(8,128)(2,1)}, u32[]{:S(2)}) copy-start(bf16[256,1536]{1,0:T(8,128)(2,1)} %copy-done.4) | copy-start | bytes 2359300 | tf_op jit(solution)/shard_map/while
  275.5 7.3 %copy-start.1 = (bf16[384,1536]{1,0:T(8,128)(2,1)S(1)}, bf16[384,1536]{1,0:T(8,128)(2,1)}, u32[]{:S(2)}) copy-start(bf16[384,1536]{1,0:T(8,128)(2,1)} %get-tuple-element.814) | copy-start | bytes 3538948 | tf_op jit(solution)/shard_map/while
  275.5 7.3 %copy-start.5 = (bf16[256,1536]{1,0:T(8,128)(2,1)S(1)}, bf16[256,1536]{1,0:T(8,128)(2,1)}, u32[]{:S(2)}) copy-start(bf16[256,1536]{1,0:T(8,128)(2,1)} %copy-done.4) | copy-start | bytes 2359300 | tf_op jit(solution)/shard_map/while
  282.8 4.3 copy-start.4
  289.8 7.3 %copy-start.1 = (bf16[384,1536]{1,0:T(8,128)(2,1)S(1)}, bf16[384,1536]{1,0:T(8,128)(2,1)}, u32[]{:S(2)}) copy-start(bf16[384,1536]{1,0:T(8,128)(2,1)} %get-tuple-element.814) | copy-start | bytes 3538948 | tf_op jit(solution)/shard_map/while
  289.8 7.3 %copy-start.5 = (bf16[256,1536]{1,0:T(8,128)(2,1)S(1)}, bf16[256,1536]{1,0:T(8,128)(2,1)}, u32[]{:S(2)}) copy-start(bf16[256,1536]{1,0:T(8,128)(2,1)} %copy-done.4) | copy-start | bytes 2359300 | tf_op jit(solution)/shard_map/while
  297.1 4.3 copy-start.4
  304.1 7.3 %copy-start.1 = (bf16[384,1536]{1,0:T(8,128)(2,1)S(1)}, bf16[384,1536]{1,0:T(8,128)(2,1)}, u32[]{:S(2)}) copy-start(bf16[384,1536]{1,0:T(8,128)(2,1)} %get-tuple-element.814) | copy-start | bytes 3538948 | tf_op jit(solution)/shard_map/while
  304.1 7.3 %copy-start.5 = (bf16[256,1536]{1,0:T(8,128)(2,1)S(1)}, bf16[256,1536]{1,0:T(8,128)(2,1)}, u32[]{:S(2)}) copy-start(bf16[256,1536]{1,0:T(8,128)(2,1)} %copy-done.4) | copy-start | bytes 2359300 | tf_op jit(solution)/shard_map/while
  318.4 7.3 %copy-start.1 = (bf16[384,1536]{1,0:T(8,128)(2,1)S(1)}, bf16[384,1536]{1,0:T(8,128)(2,1)}, u32[]{:S(2)}) copy-start(bf16[384,1536]{1,0:T(8,128)(2,1)} %get-tuple-element.814) | copy-start | bytes 3538948 | tf_op jit(solution)/shard_map/while
  318.4 7.3 %copy-start.5 = (bf16[256,1536]{1,0:T(8,128)(2,1)S(1)}, bf16[256,1536]{1,0:T(8,128)(2,1)}, u32[]{:S(2)}) copy-start(bf16[256,1536]{1,0:T(8,128)(2,1)} %copy-done.4) | copy-start | bytes 2359300 | tf_op jit(solution)/shard_map/while
  332.7 7.2 %copy-start.1 = (bf16[384,1536]{1,0:T(8,128)(2,1)S(1)}, bf16[384,1536]{1,0:T(8,128)(2,1)}, u32[]{:S(2)}) copy-start(bf16[384,1536]{1,0:T(8,128)(2,1)} %get-tuple-element.814) | copy-start | bytes 3538948 | tf_op jit(solution)/shard_map/while
  332.8 7.2 %copy-start.5 = (bf16[256,1536]{1,0:T(8,128)(2,1)S(1)}, bf16[256,1536]{1,0:T(8,128)(2,1)}, u32[]{:S(2)}) copy-start(bf16[256,1536]{1,0:T(8,128)(2,1)} %copy-done.4) | copy-start | bytes 2359300 | tf_op jit(solution)/shard_map/while
  340.0 4.3 copy-start.4
  347.0 7.3 %copy-start.1 = (bf16[384,1536]{1,0:T(8,128)(2,1)S(1)}, bf16[384,1536]{1,0:T(8,128)(2,1)}, u32[]{:S(2)}) copy-start(bf16[384,1536]{1,0:T(8,128)(2,1)} %get-tuple-element.814) | copy-start | bytes 3538948 | tf_op jit(solution)/shard_map/while
  347.0 7.3 %copy-start.5 = (bf16[256,1536]{1,0:T(8,128)(2,1)S(1)}, bf16[256,1536]{1,0:T(8,128)(2,1)}, u32[]{:S(2)}) copy-start(bf16[256,1536]{1,0:T(8,128)(2,1)} %copy-done.4) | copy-start | bytes 2359300 | tf_op jit(solution)/shard_map/while
  354.3 4.3 copy-start.4
  361.3 7.3 %copy-start.1 = (bf16[384,1536]{1,0:T(8,128)(2,1)S(1)}, bf16[384,1536]{1,0:T(8,128)(2,1)}, u32[]{:S(2)}) copy-start(bf16[384,1536]{1,0:T(8,128)(2,1)} %get-tuple-element.814) | copy-start | bytes 3538948 | tf_op jit(solution)/shard_map/while
  361.4 7.3 %copy-start.5 = (bf16[256,1536]{1,0:T(8,128)(2,1)S(1)}, bf16[256,1536]{1,0:T(8,128)(2,1)}, u32[]{:S(2)}) copy-start(bf16[256,1536]{1,0:T(8,128)(2,1)} %copy-done.4) | copy-start | bytes 2359300 | tf_op jit(solution)/shard_map/while
  368.6 4.3 copy-start.4
  375.7 7.3 %copy-start.1 = (bf16[384,1536]{1,0:T(8,128)(2,1)S(1)}, bf16[384,1536]{1,0:T(8,128)(2,1)}, u32[]{:S(2)}) copy-start(bf16[384,1536]{1,0:T(8,128)(2,1)} %get-tuple-element.814) | copy-start | bytes 3538948 | tf_op jit(solution)/shard_map/while
  375.7 7.3 %copy-start.5 = (bf16[256,1536]{1,0:T(8,128)(2,1)S(1)}, bf16[256,1536]{1,0:T(8,128)(2,1)}, u32[]{:S(2)}) copy-start(bf16[256,1536]{1,0:T(8,128)(2,1)} %copy-done.4) | copy-start | bytes 2359300 | tf_op jit(solution)/shard_map/while
  382.9 4.3 copy-start.4
  390.0 7.2 %copy-start.1 = (bf16[384,1536]{1,0:T(8,128)(2,1)S(1)}, bf16[384,1536]{1,0:T(8,128)(2,1)}, u32[]{:S(2)}) copy-start(bf16[384,1536]{1,0:T(8,128)(2,1)} %get-tuple-element.814) | copy-start | bytes 3538948 | tf_op jit(solution)/shard_map/while
  390.0 7.2 %copy-start.5 = (bf16[256,1536]{1,0:T(8,128)(2,1)S(1)}, bf16[256,1536]{1,0:T(8,128)(2,1)}, u32[]{:S(2)}) copy-start(bf16[256,1536]{1,0:T(8,128)(2,1)} %copy-done.4) | copy-start | bytes 2359300 | tf_op jit(solution)/shard_map/while
  397.2 4.3 copy-start.4
  404.3 7.3 %copy-start.1 = (bf16[384,1536]{1,0:T(8,128)(2,1)S(1)}, bf16[384,1536]{1,0:T(8,128)(2,1)}, u32[]{:S(2)}) copy-start(bf16[384,1536]{1,0:T(8,128)(2,1)} %get-tuple-element.814) | copy-start | bytes 3538948 | tf_op jit(solution)/shard_map/while
  404.3 7.3 %copy-start.5 = (bf16[256,1536]{1,0:T(8,128)(2,1)S(1)}, bf16[256,1536]{1,0:T(8,128)(2,1)}, u32[]{:S(2)}) copy-start(bf16[256,1536]{1,0:T(8,128)(2,1)} %copy-done.4) | copy-start | bytes 2359300 | tf_op jit(solution)/shard_map/while
  418.6 7.3 %copy-start.1 = (bf16[384,1536]{1,0:T(8,128)(2,1)S(1)}, bf16[384,1536]{1,0:T(8,128)(2,1)}, u32[]{:S(2)}) copy-start(bf16[384,1536]{1,0:T(8,128)(2,1)} %get-tuple-element.814) | copy-start | bytes 3538948 | tf_op jit(solution)/shard_map/while
  418.6 7.3 %copy-start.5 = (bf16[256,1536]{1,0:T(8,128)(2,1)S(1)}, bf16[256,1536]{1,0:T(8,128)(2,1)}, u32[]{:S(2)}) copy-start(bf16[256,1536]{1,0:T(8,128)(2,1)} %copy-done.4) | copy-start | bytes 2359300 | tf_op jit(solution)/shard_map/while
  458.5 110.4 %copy-start.6 = (f32[4096,12]{0,1:T(8,128)}, f32[4096,12]{0,1:T(8,128)S(1)}, u32[]{:S(2)}) copy-start(f32[4096,12]{0,1:T(8,128)S(1)} %all-gather) | copy-start | bytes 589828
  478.0 91.0 %copy-start.7 = (f32[4096,12]{0,1:T(8,128)}, f32[4096,12]{0,1:T(8,128)S(1)}, u32[]{:S(2)}) copy-start(f32[4096,12]{0,1:T(8,128)S(1)} %all-gather.1) | copy-start | bytes 589828
  572.0 16.3 %slice-start.1 = ((f32[4096,12]{0,1:T(8,128)}), f32[256,12]{0,1:T(8,128)S(1)}, s32[]{:S(2)}) async-start(f32[4096,12]{0,1:T(8,128)} %copy-done.6), calls=%async_computation.2 | async-start | bytes 32768 | tf_op jit(solution)/shard_map/slice | solution.py:52
  572.0 16.3 %slice-start.2 = ((f32[4096,12]{0,1:T(8,128)}), f32[256,12]{0,1:T(8,128)S(1)}, s32[]{:S(2)}) async-start(f32[4096,12]{0,1:T(8,128)} %copy-done.7), calls=%async_computation.3 | async-start | bytes 32768 | tf_op jit(solution)/shard_map/slice | solution.py:52
  (67 other events, 133.7 us)
Sparse Core Ops, SparseCore 0:
  426.0 142.8 all-gather.4
